TPU v7x, 32 devices: a whole 2x2x4 slice. The times are simulated.
32 devices in a mesh: wide: 2 (over x), narrow: 4 (over y, core), seq: 4 (over z).
Axes of the slice: x: 2, y: 2, z: 4, core: 2. Of those that a mesh axis runs over, the one named last changes fastest.
Arguments:
- attn_query: bfloat16 [1024, 73728], P(('seq', 'wide'), 'narrow'), parts along dimension 0, may hold values from -6 to 6
- key_latent: bfloat16 [1024, 576], P(('seq', 'wide')), parts along dimension 0, may hold values from -6 to 6
- lse_attn: float32 [128, 1024], P('narrow', ('seq', 'wide')), parts along dimension 1, may hold values from 1 to 3
- index_query: bfloat16 [1024, 8192], P(('seq', 'wide'), 'narrow'), parts along dimension 0, may hold values from -6 to 6
- index_key: bfloat16 [1024, 128], P(('seq', 'wide')), parts along dimension 0, may hold values from -6 to 6
- index_weight: float32 [64, 1024], P('narrow', ('seq', 'wide')), parts along dimension 1, may hold values from -0.75 to 0.75
- lse_index: float32 [1024], P(('seq', 'wide')), parts along dimension 0, may hold values from 0 to 1
- block_order: int32 [8], P('seq'), parts along dimension 0, may hold values from 0 to 127, as said below
Outputs:
- d_index_query: float32 [1024, 8192], P(('seq', 'wide'), 'narrow'), parts along dimension 0
- d_index_weight: float32 [64, 1024], P('narrow', ('seq', 'wide')), parts along dimension 1
- d_index_key: float32 [1024, 128], P(('seq', 'wide')), parts along dimension 0
There are 4 independent parts, one for each index of `seq`. A program takes and returns all parts, laid end to end along the dimension named above; each array names one. Nothing has to cross between parts.
Inputs may be any that keep to these rules, and one draw needn't show every extreme that they name: Index d of wide holds tokens 128 * block_order[d] to 128 * block_order[d] + 127 of the context; the values are distinct.
All inputs are finite; a program needn't handle non-finite values.
Results may differ from a plain program's by a relative error of at most 0.008.
Values may be sent and summed in bfloat16 or wider, within the bound.
No kernel may reach another device: no remote copies, remote signals or barrier semaphores. Data moves between devices by JAX's collectives and lax.ppermute only.
A program may use at most 64 MiB of HBM per device.

v0:
```python
import jax
import jax.numpy as jnp
from jax import lax
from jax.sharding import PartitionSpec as P

HEADS = 128
attn_scale = 192.0 ** (-0.5)


def shifted(block, axis, distance):
    devices = range(lax.axis_size(axis))
    route = [((i - distance) % len(devices), i) for i in devices]
    return lax.ppermute(block, axis, route)


def body(
    attn_query, key_latent, lse_attn, index_query, index_key, index_weight, lse_index, block_order
):
    tok_rows = key_latent.shape[0]
    key_width = key_latent.shape[1]
    index_width = index_key.shape[1]
    heads_here = attn_query.shape[1] // key_width
    iheads_here = index_query.shape[1] // index_width
    cycle_size = lax.axis_size("wide")
    cycle_place = lax.axis_index("wide")
    query_heads = attn_query.reshape(tok_rows, heads_here, key_width)
    index_heads = index_query.reshape(tok_rows, iheads_here, index_width)
    offsets = jnp.arange(tok_rows, dtype=jnp.int32)
    query_pos = block_order[cycle_place] * tok_rows + offsets
    lse_rows = jnp.transpose(lse_attn)
    weight_rows = jnp.transpose(index_weight)
    index_scale = index_width ** (-0.5)

    def block_grads(key_block, ikey_block, source):
        key_pos = block_order[source] * tok_rows + offsets
        causal = query_pos[:, None] >= key_pos[None, :]
        scores = (
            jnp.einsum("thc,sc->ths", query_heads, key_block, preferred_element_type=jnp.float32)
            * attn_scale
        )
        part_target = jnp.sum(jnp.exp(scores - lse_rows[:, :, None]), axis=1) / HEADS
        logits = (
            jnp.einsum("tjc,sc->tjs", index_heads, ikey_block, preferred_element_type=jnp.float32)
            * index_scale
        )
        active = jnp.maximum(logits, 0.0)
        part_score = jnp.einsum("tjs,tj->ts", active, weight_rows)
        target, score = lax.psum((part_target, part_score), "narrow")
        difference = jnp.where(causal, jnp.exp(score - lse_index[:, None]) - target, 0.0)
        grad_weight = jnp.einsum("ts,tjs->tj", difference, active)
        coefficient = (
            difference[:, None, :]
            * weight_rows[:, :, None]
            * (logits > 0.0).astype(jnp.float32)
            * index_scale
        ).astype(jnp.bfloat16)
        grad_query = jnp.einsum(
            "tjs,sc->tjc", coefficient, ikey_block, preferred_element_type=jnp.float32
        )
        grad_key = jnp.einsum(
            "tjs,tjc->sc", coefficient, index_heads, preferred_element_type=jnp.float32
        )
        return (grad_query, grad_weight, grad_key)

    def move_keys(key_block, ikey_block):
        return shifted((key_block, ikey_block), "wide", 1)

    zero_query = jnp.zeros((tok_rows, iheads_here, index_width), jnp.float32)
    zero_weight = jnp.zeros((tok_rows, iheads_here), jnp.float32)
    last_source = (cycle_place + 1) % cycle_size

    def pass_grad(carried):
        return shifted(carried, "wide", 1)

    def cycle_step(step_index, carried_state):
        key_block, ikey_block, carried, sum_query, sum_weight = carried_state
        source = (cycle_place - step_index) % cycle_size
        grad_query, grad_weight, grad_key = block_grads(key_block, ikey_block, source)
        key_block, ikey_block = move_keys(key_block, ikey_block)
        return (
            key_block,
            ikey_block,
            pass_grad(carried + grad_key),
            sum_query + grad_query,
            sum_weight + grad_weight,
        )

    start_state = (
        key_latent,
        index_key,
        jnp.zeros((tok_rows, index_width), jnp.float32),
        zero_query,
        zero_weight,
    )
    key_block, ikey_block, carried, sum_query, sum_weight = lax.fori_loop(
        0, cycle_size - 1, cycle_step, start_state
    )
    grad_query, grad_weight, grad_key = block_grads(key_block, ikey_block, last_source)
    own_key = pass_grad(carried + grad_key)
    key_total = lax.psum(own_key, "narrow")
    sum_query = sum_query + grad_query
    sum_weight = sum_weight + grad_weight
    return (
        sum_query.reshape(tok_rows, iheads_here * index_width),
        jnp.transpose(sum_weight),
        key_total,
    )


def solution(mesh):
    in_specs = (
        P(("seq", "wide"), "narrow"),
        P(("seq", "wide"), None),
        P("narrow", ("seq", "wide")),
        P(("seq", "wide"), "narrow"),
        P(("seq", "wide"), None),
        P("narrow", ("seq", "wide")),
        P(("seq", "wide")),
        P("seq"),
    )
    out_specs = (
        P(("seq", "wide"), "narrow"),
        P("narrow", ("seq", "wide")),
        P(("seq", "wide"), None),
    )
    return jax.shard_map(body, mesh=mesh, in_specs=in_specs, out_specs=out_specs, check_vma=False)
```

profile of v0, /device:TPU:0, one launch (start us, length us, event | category | flops | bytes accessed | tf_op | source)
XLA Modules:
  0.0 119.6 jit_solution(2977630586859763670)
XLA Ops:
  7.2 3.0 %collective-permute-start = (bf16[128,128]{1,0:T(8,128)(2,1)}, bf16[128,128]{1,0:T(8,128)(2,1)S(1)}, u32[]{:S(2)}, u32[]{:S(2)}) collective-permute-start(bf16[128,128]{1,0:T(8,128)(2,1)} %param.12), channel_id=1, source_target_pairs={{16,0},{0,16},{17,1},{1,17},{18,2},{2,18},{19,3},{3,19},{20,4},{4,... | collective-permute-start | bytes 98312 | tf_op jit(solution)/shard_map/while/body/eval_jaxpr/ppermute | solution.py:13
  10.3 1.4 %fusion.43 = (s32[1]{0:T(128)}, s32[1]{0:T(128)}, s32[1]{0:T(128)}) fusion(s32[2]{0:T(128)} %param.15, s32[]{:T(128)S(6)} %select_n.36, s32[]{:T(128)S(6)} %select_n.31, s32[]{:T(128)S(6)} %select_n.33), kind=kLoop, calls=%fused_computation.67 | loop fusion | bytes 36 | tf_op jit(solution)/shard_map/dynamic_slice | solution.py:35
  13.6 0.8 copy.33
  14.5 1.1 broadcast_maximum_fusion.1
  15.7 6.7 %copy.23 = bf16[128,18432]{0,1:T(8,128)(2,1)} copy(bf16[128,18432]{1,0:T(8,128)(2,1)} %param.8) | data formatting | bytes 9437184 | tf_op args[0]
  22.4 4.5 %exponential_reduce_fusion.1 = f32[128,128]{1,0:T(8,128)S(1)} fusion(bf16[128,32,576]{0,2,1:T(8,128)(2,1)} %bitcast.87, f32[128,32]{0,1:T(8,128)S(1)} %bitcast.101, bf16[128,576]{0,1:T(8,128)(2,1)S(1)} %copy-done.5), kind=kOutput, calls=%fused_computation.1 | convolution fusion | flops 605536256 | bytes 4947968 | tf_op jit(solution)/shard_map/while/body/eval_jaxpr/thc,sc->ths/dot_general | solution.py:38
  26.9 0.6 broadcast_multiply_fusion.1
  27.6 1.1 fusion.7
  29.0 1.1 fusion.3
  30.0 2.2 %exponential_reduce_fusion = f32[128,128]{1,0:T(8,128)S(1)} fusion(bf16[128,32,576]{0,2,1:T(8,128)(2,1)S(1)} %bitcast.90, f32[128,32]{0,1:T(8,128)S(1)} %bitcast.102, bf16[128,576]{0,1:T(8,128)(2,1)S(1)} %collective-permute-done.1), kind=kOutput, calls=%fused_computation | convolution fusion | flops 605536256 | bytes 4947968 | tf_op jit(solution)/shard_map/thc,sc->ths/dot_general | solution.py:38
  32.2 0.6 broadcast_multiply_fusion
  33.1 34.1 %all-reduce.6.cloned.1.call-done = (f32[128,128]{1,0:T(8,128)}, f32[128,128]{1,0:T(8,128)}, f32[128,128]{1,0:T(8,128)}, f32[128,128]{1,0:T(8,128)}) async-done(((f32[128,128]{1,0:T(8,128)}, f32[128,128]{1,0:T(8,128)}, f32[128,128]{1,0:T(8,128)}, f32[128,128]{1,0:T(8,128)}), (f32[128,128]{1,0:T(8,128)}, f32[128,128]{1,0:T(8,128)}, f32[128,128]{1,0:T(8,128)}, ...) | async-done | bytes 262160 | tf_op jit(solution)/shard_map/while/body/eval_jaxpr/psum | solution.py:48
  67.2 1.0 subtract_select_fusion
  68.3 0.7 convolution_bitcast_fusion.1
  69.6 1.5 %collective-permute-start.2 = (f32[128,128]{1,0:T(8,128)S(1)}, f32[128,128]{1,0:T(8,128)S(1)}, u32[]{:S(2)}, u32[]{:S(2)}) collective-permute-start(f32[128,128]{1,0:T(8,128)S(1)} %convolution_bitcast_fusion.1), channel_id=1, source_target_pairs={{16,0},{0,16},{17,1},{1,17},{18,2},{2,18},{19,3},{3,19},{20,4},{4,... | collective-permute-start | bytes 196616 | tf_op jit(solution)/shard_map/while/body/eval_jaxpr/ppermute | solution.py:13
  72.1 1.8 %collective-permute-done.2 = f32[128,128]{1,0:T(8,128)S(1)} collective-permute-done((f32[128,128]{1,0:T(8,128)S(1)}, f32[128,128]{1,0:T(8,128)S(1)}, u32[]{:S(2)}, u32[]{:S(2)}) %collective-permute-start.2) | collective-permute-done | bytes 65568 | tf_op jit(solution)/shard_map/while/body/eval_jaxpr/ppermute | solution.py:13
  73.9 0.7 fusion
  74.6 1.5 %collective-permute-start.3 = (f32[128,128]{1,0:T(8,128)S(1)}, f32[128,128]{1,0:T(8,128)S(1)}, u32[]{:S(2)}, u32[]{:S(2)}) collective-permute-start(f32[128,128]{1,0:T(8,128)S(1)} %fusion), channel_id=1, source_target_pairs={{16,0},{0,16},{17,1},{1,17},{18,2},{2,18},{19,3},{3,19},{20,4},{4,... | collective-permute-start | bytes 196616 | tf_op jit(solution)/shard_map/ppermute | solution.py:13
  76.7 2.2 %collective-permute-done.3 = f32[128,128]{1,0:T(8,128)S(1)} collective-permute-done((f32[128,128]{1,0:T(8,128)S(1)}, f32[128,128]{1,0:T(8,128)S(1)}, u32[]{:S(2)}, u32[]{:S(2)}) %collective-permute-start.3) | collective-permute-done | bytes 65568 | tf_op jit(solution)/shard_map/ppermute | solution.py:13
  79.0 0.6 copy-done.1
  79.6 0.6 fusion.30
  80.2 1.3 %copy.31 = f32[128,2048]{1,0:T(8,128)} copy(f32[128,2048]{0,1:T(8,128)S(1)} %bitcast.91) | data formatting | bytes 2097152
  81.5 29.8 %all-reduce.4.cloned.1.call-done = f32[128,128]{1,0:T(8,128)} async-done(((f32[128,128]{1,0:T(8,128)}), f32[128,128]{1,0:T(8,128)}) %all-reduce.4.cloned.1.call-update) | async-done | bytes 65552 | tf_op jit(solution)/shard_map/psum | solution.py:100
  111.3 1.5 %copy.82 = f32[128,128]{1,0:T(8,128)} copy(f32[128,128]{1,0:T(8,128)} %all-reduce.4.cloned.1.call-done) | data formatting | bytes 131072
  (36 shorter events, 3.0 us)
Async XLA Ops:
  7.2 7.3 %copy-start = (bf16[128,2048]{1,0:T(8,128)(2,1)S(1)}, bf16[128,2048]{1,0:T(8,128)(2,1)}, u32[]{:S(2)}) copy-start(bf16[128,2048]{1,0:T(8,128)(2,1)} %param.11) | copy-start | bytes 1572868
  7.2 60.0 %all-reduce.6.cloned.1.call-start = ((), (), s32[]{:S(2)}) async-start(), calls=%async_computation.1 | async-start | bytes 524288 | tf_op jit(solution)/shard_map/while/body/eval_jaxpr/psum | solution.py:48
  7.2 21.4 %collective-permute-start = (bf16[128,128]{1,0:T(8,128)(2,1)}, bf16[128,128]{1,0:T(8,128)(2,1)S(1)}, u32[]{:S(2)}, u32[]{:S(2)}) collective-permute-start(bf16[128,128]{1,0:T(8,128)(2,1)} %param.12), channel_id=1, source_target_pairs={{16,0},{0,16},{17,1},{1,17},{18,2},{2,18},{19,3},{3,19},{20,4},{4,... | collective-permute-start | bytes 98312 | tf_op jit(solution)/shard_map/while/body/eval_jaxpr/ppermute | solution.py:13
  10.3 19.8 %collective-permute-start.1 = (bf16[128,576]{0,1:T(8,128)(2,1)}, bf16[128,576]{0,1:T(8,128)(2,1)S(1)}, u32[]{:S(2)}, u32[]{:S(2)}) collective-permute-start(bf16[128,576]{0,1:T(8,128)(2,1)} %param.9), channel_id=1, source_target_pairs={{16,0},{0,16},{17,1},{1,17},{18,2},{2,18},{19,3},{3,19},{20,4},{4,... | collective-permute-start | bytes 442376 | tf_op jit(solution)/shard_map/while/body/eval_jaxpr/ppermute | solution.py:13
  15.7 6.7 %copy-start.5 = (bf16[128,576]{0,1:T(8,128)(2,1)S(1)}, bf16[128,576]{0,1:T(8,128)(2,1)}, u32[]{:S(2)}) copy-start(bf16[128,576]{0,1:T(8,128)(2,1)} %param.9) | copy-start | bytes 442372
  15.7 6.7 %copy-start.6 = (f32[32,128]{1,0:T(8,128)S(1)}, f32[32,128]{1,0:T(8,128)}, u32[]{:S(2)}) copy-start(f32[32,128]{1,0:T(8,128)} %param.10) | copy-start | bytes 49156
  22.4 7.6 %slice-start = ((s8[4718592]{0:T(1024)(128)(4,1)}), s8[4194304]{0:T(1024)(128)(4,1)S(1)}, s32[]{:S(2)}) async-start(s8[4718592]{0:T(1024)(128)(4,1)} %bitcast.88), calls=%async_computation.2 | async-start | bytes 8388608
  22.4 7.6 %slice-start.1 = ((s8[4718592]{0:T(1024)(128)(4,1)}), s8[524288]{0:T(1024)(128)(4,1)S(1)}, s32[]{:S(2)}) async-start(s8[4718592]{0:T(1024)(128)(4,1)} %bitcast.88), calls=%async_computation.3 | async-start | bytes 1048576
  30.0 37.2 %copy-start.4 = (f32[128]{0:T(128)S(1)}, f32[128]{0:T(128)}, u32[]{:S(2)}) copy-start(f32[128]{0:T(128)} %param.14) | copy-start | bytes 1540
  30.0 38.3 %copy-start.3 = (f32[16,128]{1,0:T(8,128)S(1)}, f32[16,128]{1,0:T(8,128)}, u32[]{:S(2)}) copy-start(f32[16,128]{1,0:T(8,128)} %param.13) | copy-start | bytes 24580
  32.9 78.4 %all-reduce.4.cloned.1.call-start = ((), (), s32[]{:S(2)}) async-start(), calls=%async_computation | async-start | bytes 131072 | tf_op jit(solution)/shard_map/psum | solution.py:100
  32.9 36.1 %copy-start.2 = (bf16[128,128]{1,0:T(8,128)(2,1)S(1)}, bf16[128,128]{1,0:T(8,128)(2,1)}, u32[]{:S(2)}) copy-start(bf16[128,128]{1,0:T(8,128)(2,1)} %param.12) | copy-start | bytes 98308
  69.6 4.3 %collective-permute-start.2 = (f32[128,128]{1,0:T(8,128)S(1)}, f32[128,128]{1,0:T(8,128)S(1)}, u32[]{:S(2)}, u32[]{:S(2)}) collective-permute-start(f32[128,128]{1,0:T(8,128)S(1)} %convolution_bitcast_fusion.1), channel_id=1, source_target_pairs={{16,0},{0,16},{17,1},{1,17},{18,2},{2,18},{19,3},{3,19},{20,4},{4,... | collective-permute-start | bytes 196616 | tf_op jit(solution)/shard_map/while/body/eval_jaxpr/ppermute | solution.py:13
  74.6 4.3 %collective-permute-start.3 = (f32[128,128]{1,0:T(8,128)S(1)}, f32[128,128]{1,0:T(8,128)S(1)}, u32[]{:S(2)}, u32[]{:S(2)}) collective-permute-start(f32[128,128]{1,0:T(8,128)S(1)} %fusion), channel_id=1, source_target_pairs={{16,0},{0,16},{17,1},{1,17},{18,2},{2,18},{19,3},{3,19},{20,4},{4,... | collective-permute-start | bytes 196616 | tf_op jit(solution)/shard_map/ppermute | solution.py:13
  79.0 0.6 copy-start.1
Sparse Core Ops, SparseCore 0:
  33.0 34.1 all-reduce.5
  79.7 31.5 all-reduce.3
where the time goes:
time: 120 us
  waiting for transfers between devices  67.9 us (57%)
  between operations  16.2 us (14%)
  matrix products  13.6 us (11%)
  local copies, waits for them, and re-layouts  12.4 us (10%)
  starting transfers between devices  6.27 us (5%)
  other arithmetic  3.2 us (3%)
    psum x1, waiting for transfers between devices, block_grads(): target, score = lax.psum((part_target, part_score), 'narrow')  34.1 us
    psum x1, waiting for transfers between devices, body(): key_total = lax.psum(own_key, 'narrow')  29.8 us
    unnamed x21, local copies, waits for them, and re-layouts  10.1 us
    dot_general x2, matrix products, block_grads(): jnp.einsum('thc,sc->ths', query_heads, key_block, preferred_element_type=...  6.66 us
    ppermute x4, starting transfers between devices, shifted(): return lax.ppermute(block, axis, route)  6.19 us
    ppermute x4, waiting for transfers between devices, shifted(): return lax.ppermute(block, axis, route)  4 us
  transfers between devices with their start and end apart: 6, of which 4 were waited for; matrix products, arithmetic and copies ran while one was open for 18% of the time, Pallas kernels for 0%

commit v1 on v0

--- a/solution.py
+++ b/solution.py
@@ -97,7 +97,8 @@
     )
     grad_query, grad_weight, grad_key = block_grads(key_block, ikey_block, last_source)
     own_key = pass_grad(carried + grad_key)
-    key_total = lax.psum(own_key, "narrow")
+    _push_terms = lambda local: jnp.sum(lax.all_gather(local, "narrow"), axis=0)
+    key_total = _push_terms(own_key)
     sum_query = sum_query + grad_query
     sum_weight = sum_weight + grad_weight
     return (

time: 120 us -> 93.1 us (0.78)
  waiting for transfers between devices: 67.9 us -> 36.8 us
  blocking collectives: 0 us -> 5.76 us
  local copies, waits for them, and re-layouts: 12.4 us -> 10.3 us
    psum x1 -> x0, waiting for transfers between devices: 29.8 us -> none  [body(): key_total = lax.psum(own_key, 'narrow')]
    all_gather x0 -> x1, blocking collectives: none -> 5.76 us  [body(): _push_terms = lambda local: jnp.sum(lax.all_gather(local, 'narrow'), axis=0)]
    unnamed x21 -> x18, local copies, waits for them, and re-layouts: 10.1 us -> 8.02 us
    ppermute x4, waiting for transfers between devices: 4 us -> 2.54 us  [shifted(): return lax.ppermute(block, axis, route)]
  transfers between devices with their start and end apart: 6 -> 5, of which waited for: 4 -> 3; matrix products, arithmetic and copies ran while one was open for 18% -> 23% of each run, Pallas kernels for 0% -> 0%
where the time goes in v1:
time: 93.1 us; the launch traced here: 92.7 us
  waiting for transfers between devices  36.8 us (40%)
  between operations  16.1 us (17%)
  matrix products  13.6 us (15%)
  local copies, waits for them, and re-layouts  10.3 us (11%)
  starting transfers between devices  6.19 us (7%)
  blocking collectives  5.76 us (6%)
  other arithmetic  3.83 us (4%)
    psum x1, waiting for transfers between devices, block_grads(): target, score = lax.psum((part_target, part_score), 'narrow')  34.2 us
    unnamed x18, local copies, waits for them, and re-layouts  8.02 us
    dot_general x2, matrix products, block_grads(): jnp.einsum('thc,sc->ths', query_heads, key_block, preferred_element_type=...  6.67 us
    ppermute x4, starting transfers between devices, shifted(): return lax.ppermute(block, axis, route)  6.15 us
    all_gather x1, blocking collectives, body(): _push_terms = lambda local: jnp.sum(lax.all_gather(local, 'narrow'), axis=0)  5.76 us
    ppermute x4, waiting for transfers between devices, shifted(): return lax.ppermute(block, axis, route)  2.54 us
    dot_general x2, matrix products, block_grads(): part_score = jnp.einsum('tjs,tj->ts', active, weight_rows)  2.13 us
  transfers between devices with their start and end apart: 5, of which 3 were waited for; matrix products, arithmetic and copies ran while one was open for 23% of the time, Pallas kernels for 0%

profile of v1, /device:TPU:0, one launch (start us, length us, event | category | flops | bytes accessed | tf_op | source)
XLA Modules:
  0.0 92.7 jit_solution(16701534698627602260)
XLA Ops:
  7.2 3.0 %collective-permute-start = (bf16[128,128]{1,0:T(8,128)(2,1)}, bf16[128,128]{1,0:T(8,128)(2,1)S(1)}, u32[]{:S(2)}, u32[]{:S(2)}) collective-permute-start(bf16[128,128]{1,0:T(8,128)(2,1)} %param.12), channel_id=1, source_target_pairs={{16,0},{0,16},{17,1},{1,17},{18,2},{2,18},{19,3},{3,19},{20,4},{4,... | collective-permute-start | bytes 98312 | tf_op jit(solution)/shard_map/while/body/eval_jaxpr/ppermute | solution.py:13
  10.3 1.4 %fusion.43 = (s32[1]{0:T(128)}, s32[1]{0:T(128)}, s32[1]{0:T(128)}) fusion(s32[2]{0:T(128)} %param.15, s32[]{:T(128)S(6)} %select_n.36, s32[]{:T(128)S(6)} %select_n.31, s32[]{:T(128)S(6)} %select_n.33), kind=kLoop, calls=%fused_computation.67 | loop fusion | bytes 36 | tf_op jit(solution)/shard_map/dynamic_slice | solution.py:35
  13.6 0.8 copy.33
  14.5 1.1 %broadcast_maximum_fusion.1 = (bf16[128,16,128]{2,0,1:T(8,128)(2,1)S(1)}, f32[128,16,128]{2,0,1:T(8,128)S(1)}) fusion(bf16[128,128]{1,0:T(8,128)(2,1)} %param.12, bf16[128,2048]{1,0:T(8,128)(2,1)S(1)} %copy-done), kind=kOutput, calls=%fused_computation.30 | convolution fusion | flops 67895296 | bytes 2129920 | tf_op jit(solution)/shard_map/while/body/eval_jaxpr/tjc,sc->tjs/dot_general | solution.py:43
  15.7 6.7 %copy.23 = bf16[128,18432]{0,1:T(8,128)(2,1)} copy(bf16[128,18432]{1,0:T(8,128)(2,1)} %param.8) | data formatting | bytes 9437184 | tf_op args[0]
  22.4 4.5 %exponential_reduce_fusion.1 = f32[128,128]{1,0:T(8,128)S(1)} fusion(bf16[128,32,576]{0,2,1:T(8,128)(2,1)} %bitcast.88, f32[128,32]{0,1:T(8,128)S(1)} %bitcast.103, bf16[128,576]{0,1:T(8,128)(2,1)S(1)} %copy-done.4), kind=kOutput, calls=%fused_computation.1 | convolution fusion | flops 605536256 | bytes 4947968 | tf_op jit(solution)/shard_map/while/body/eval_jaxpr/thc,sc->ths/dot_general | solution.py:38
  26.9 0.6 broadcast_multiply_fusion.1
  27.6 1.1 %fusion.7 = f32[128,1,128]{2,1,0:T(1,128)} fusion(bf16[128,16,1]{1,2,0:T(2,128)(2,1)S(1)} %copy.33, bf16[128,16,128]{2,0,1:T(8,128)(2,1)S(1)} %get-tuple-element.66), kind=kOutput, calls=%fused_computation.21 | convolution fusion | flops 524288 | bytes 593920 | tf_op jit(solution)/shard_map/while/body/eval_jaxpr/tjs,tj->ts/dot_general | solution.py:47
  29.0 1.1 %fusion.3 = f32[128,1,128]{2,1,0:T(1,128)} fusion(bf16[128,16,1]{1,2,0:T(2,128)(2,1)S(1)} %copy.33, bf16[128,16,128]{2,0,1:T(8,128)(2,1)S(1)} %get-tuple-element.68), kind=kOutput, calls=%fused_computation.17 | convolution fusion | flops 524288 | bytes 593920 | tf_op jit(solution)/shard_map/tjs,tj->ts/dot_general | solution.py:47
  30.1 2.2 %exponential_reduce_fusion = f32[128,128]{1,0:T(8,128)S(1)} fusion(bf16[128,32,576]{0,2,1:T(8,128)(2,1)S(1)} %bitcast.91, f32[128,32]{0,1:T(8,128)S(1)} %bitcast.104, bf16[128,576]{0,1:T(8,128)(2,1)S(1)} %collective-permute-done.1), kind=kOutput, calls=%fused_computation | convolution fusion | flops 605536256 | bytes 4947968 | tf_op jit(solution)/shard_map/thc,sc->ths/dot_general | solution.py:38
  32.2 0.6 broadcast_multiply_fusion
  33.1 34.2 %all-reduce.3.cloned.1.call-done = (f32[128,128]{1,0:T(8,128)}, f32[128,128]{1,0:T(8,128)}, f32[128,128]{1,0:T(8,128)}, f32[128,128]{1,0:T(8,128)}) async-done(((f32[128,128]{1,0:T(8,128)}, f32[128,128]{1,0:T(8,128)}, f32[128,128]{1,0:T(8,128)}, f32[128,128]{1,0:T(8,128)}), (f32[128,128]{1,0:T(8,128)}, f32[128,128]{1,0:T(8,128)}, f32[128,128]{1,0:T(8,128)}, ...) | async-done | bytes 262160 | tf_op jit(solution)/shard_map/while/body/eval_jaxpr/psum | solution.py:48
  67.3 1.0 %subtract_select_fusion = (f32[128,128]{1,0:T(8,128)S(1)}, f32[128,128]{1,0:T(8,128)S(1)}) fusion(f32[128,128]{1,0:T(8,128)} %get-tuple-element.43, f32[128,128]{1,0:T(8,128)} %get-tuple-element.44, s32[128]{0:T(128)S(1)} %get-tuple-element.70, f32[128]{0:T(128)S(1)} %copy-done.3, s32[128]{0:T(128)S(1)} %iota_add_fusion.2, f32[128,128]{1,0:T(8,128)} %get-tuple-element.41, ...), kind=kLoop, calls=%fused_computation.42 | loop fusion | flops 131072 | bytes 395264 | tf_op jit(solution)/shard_map/jit(_where)/select_n | solution.py:49
  68.3 0.7 convolution_bitcast_fusion.1
  69.0 0.6 fusion.15
  70.0 1.5 %collective-permute-start.2 = (f32[128,128]{1,0:T(8,128)S(1)}, f32[128,128]{1,0:T(8,128)S(1)}, u32[]{:S(2)}, u32[]{:S(2)}) collective-permute-start(f32[128,128]{1,0:T(8,128)S(1)} %convolution_bitcast_fusion.1), channel_id=1, source_target_pairs={{16,0},{0,16},{17,1},{1,17},{18,2},{2,18},{19,3},{3,19},{20,4},{4,... | collective-permute-start | bytes 196616 | tf_op jit(solution)/shard_map/while/body/eval_jaxpr/ppermute | solution.py:13
  72.7 1.6 %collective-permute-done.2 = f32[128,128]{1,0:T(8,128)S(1)} collective-permute-done((f32[128,128]{1,0:T(8,128)S(1)}, f32[128,128]{1,0:T(8,128)S(1)}, u32[]{:S(2)}, u32[]{:S(2)}) %collective-permute-start.2) | collective-permute-done | bytes 65568 | tf_op jit(solution)/shard_map/while/body/eval_jaxpr/ppermute | solution.py:13
  74.4 0.7 fusion
  75.1 1.5 %collective-permute-start.3 = (f32[128,128]{1,0:T(8,128)S(1)}, f32[128,128]{1,0:T(8,128)S(1)}, u32[]{:S(2)}, u32[]{:S(2)}) collective-permute-start(f32[128,128]{1,0:T(8,128)S(1)} %fusion), channel_id=1, source_target_pairs={{16,0},{0,16},{17,1},{1,17},{18,2},{2,18},{19,3},{3,19},{20,4},{4,... | collective-permute-start | bytes 196616 | tf_op jit(solution)/shard_map/ppermute | solution.py:13
  76.6 0.6 fusion.30
  77.2 1.3 %copy.31 = f32[128,2048]{1,0:T(8,128)} copy(f32[128,2048]{0,1:T(8,128)S(1)} %bitcast.93) | data formatting | bytes 2097152
  78.5 0.9 collective-permute-done.3
  79.4 5.8 %all-gather = f32[512,128]{1,0:T(8,128)S(1)} all-gather(f32[128,128]{1,0:T(8,128)S(1)} %collective-permute-done.3), channel_id=2, replica_groups=mesh['wide'=2,'narrow'=4,'seq'=4] {'narrow'}, dimensions={0}, use_global_device_ids=true | all-gather | bytes 327680 | tf_op jit(solution)/shard_map/all_gather | solution.py:100
  85.2 0.6 reduce_sum.30
  (32 shorter events, 2.4 us)
Async XLA Ops:
  7.2 7.3 %copy-start = (bf16[128,2048]{1,0:T(8,128)(2,1)S(1)}, bf16[128,2048]{1,0:T(8,128)(2,1)}, u32[]{:S(2)}) copy-start(bf16[128,2048]{1,0:T(8,128)(2,1)} %param.11) | copy-start | bytes 1572868
  7.2 60.1 %all-reduce.3.cloned.1.call-start = ((), (), s32[]{:S(2)}) async-start(), calls=%async_computation | async-start | bytes 524288 | tf_op jit(solution)/shard_map/while/body/eval_jaxpr/psum | solution.py:48
  7.2 21.4 %collective-permute-start = (bf16[128,128]{1,0:T(8,128)(2,1)}, bf16[128,128]{1,0:T(8,128)(2,1)S(1)}, u32[]{:S(2)}, u32[]{:S(2)}) collective-permute-start(bf16[128,128]{1,0:T(8,128)(2,1)} %param.12), channel_id=1, source_target_pairs={{16,0},{0,16},{17,1},{1,17},{18,2},{2,18},{19,3},{3,19},{20,4},{4,... | collective-permute-start | bytes 98312 | tf_op jit(solution)/shard_map/while/body/eval_jaxpr/ppermute | solution.py:13
  10.3 19.8 %collective-permute-start.1 = (bf16[128,576]{0,1:T(8,128)(2,1)}, bf16[128,576]{0,1:T(8,128)(2,1)S(1)}, u32[]{:S(2)}, u32[]{:S(2)}) collective-permute-start(bf16[128,576]{0,1:T(8,128)(2,1)} %param.9), channel_id=1, source_target_pairs={{16,0},{0,16},{17,1},{1,17},{18,2},{2,18},{19,3},{3,19},{20,4},{4,... | collective-permute-start | bytes 442376 | tf_op jit(solution)/shard_map/while/body/eval_jaxpr/ppermute | solution.py:13
  15.7 6.7 %copy-start.4 = (bf16[128,576]{0,1:T(8,128)(2,1)S(1)}, bf16[128,576]{0,1:T(8,128)(2,1)}, u32[]{:S(2)}) copy-start(bf16[128,576]{0,1:T(8,128)(2,1)} %param.9) | copy-start | bytes 442372
  15.7 6.7 %copy-start.5 = (f32[32,128]{1,0:T(8,128)S(1)}, f32[32,128]{1,0:T(8,128)}, u32[]{:S(2)}) copy-start(f32[32,128]{1,0:T(8,128)} %param.10) | copy-start | bytes 49156
  22.4 7.6 %slice-start = ((s8[4718592]{0:T(1024)(128)(4,1)}), s8[4194304]{0:T(1024)(128)(4,1)S(1)}, s32[]{:S(2)}) async-start(s8[4718592]{0:T(1024)(128)(4,1)} %bitcast.89), calls=%async_computation.1 | async-start | bytes 8388608
  22.4 7.6 %slice-start.1 = ((s8[4718592]{0:T(1024)(128)(4,1)}), s8[524288]{0:T(1024)(128)(4,1)S(1)}, s32[]{:S(2)}) async-start(s8[4718592]{0:T(1024)(128)(4,1)} %bitcast.89), calls=%async_computation.2 | async-start | bytes 1048576
  30.0 37.2 %copy-start.3 = (f32[128]{0:T(128)S(1)}, f32[128]{0:T(128)}, u32[]{:S(2)}) copy-start(f32[128]{0:T(128)} %param.14) | copy-start | bytes 1540
  30.0 38.3 %copy-start.2 = (f32[16,128]{1,0:T(8,128)S(1)}, f32[16,128]{1,0:T(8,128)}, u32[]{:S(2)}) copy-start(f32[16,128]{1,0:T(8,128)} %param.13) | copy-start | bytes 24580
  32.9 36.1 %copy-start.1 = (bf16[128,128]{1,0:T(8,128)(2,1)S(1)}, bf16[128,128]{1,0:T(8,128)(2,1)}, u32[]{:S(2)}) copy-start(bf16[128,128]{1,0:T(8,128)(2,1)} %param.12) | copy-start | bytes 98308
  70.0 4.3 %collective-permute-start.2 = (f32[128,128]{1,0:T(8,128)S(1)}, f32[128,128]{1,0:T(8,128)S(1)}, u32[]{:S(2)}, u32[]{:S(2)}) collective-permute-start(f32[128,128]{1,0:T(8,128)S(1)} %convolution_bitcast_fusion.1), channel_id=1, source_target_pairs={{16,0},{0,16},{17,1},{1,17},{18,2},{2,18},{19,3},{3,19},{20,4},{4,... | collective-permute-start | bytes 196616 | tf_op jit(solution)/shard_map/while/body/eval_jaxpr/ppermute | solution.py:13
  75.1 4.3 %collective-permute-start.3 = (f32[128,128]{1,0:T(8,128)S(1)}, f32[128,128]{1,0:T(8,128)S(1)}, u32[]{:S(2)}, u32[]{:S(2)}) collective-permute-start(f32[128,128]{1,0:T(8,128)S(1)} %fusion), channel_id=1, source_target_pairs={{16,0},{0,16},{17,1},{1,17},{18,2},{2,18},{19,3},{3,19},{20,4},{4,... | collective-permute-start | bytes 196616 | tf_op jit(solution)/shard_map/ppermute | solution.py:13
Sparse Core Ops, SparseCore 0:
  33.0 34.1 all-reduce.2
